TPU v7x, 32 devices: a whole 2x2x4 slice. The times are simulated.
32 devices in a mesh: samp: 4 (over x, core), snp: 4 (over z), gene: 2 (over y).
Axes of the slice: x: 2, y: 2, z: 4, core: 2. Of those that a mesh axis runs over, the one named last changes fastest.
Arguments:
- dosage: bfloat16 [18432, 1024], P(('samp', 'gene'), 'snp'), may hold values from 0 to 2
- snp_scale: float32 [1024], P('snp'), may hold values from 0.5 to 2
- covariates: float32 [18432, 64], P(('samp', 'gene'))
- previous: bfloat16 [18432, 1024], P(('samp', 'gene'), 'snp')
- expression: bfloat16 [18432, 20480], P('samp', 'gene')
Outputs:
- resid: bfloat16 [18432, 1024], P(('samp', 'gene'), 'snp')
- zscores: bfloat16 [1024, 20480], P('snp', 'gene')
All inputs are finite; a program needn't handle non-finite values.
Results may differ from a plain program's by a relative error of at most 0.001.
Values may be sent and summed in bfloat16 or wider, within the bound.
No kernel may reach another device: no remote copies, remote signals or barrier semaphores. Data moves between devices by JAX's collectives and lax.ppermute only.
A program may use at most 192 MiB of HBM per device.

v0:
```python
import jax
import jax.numpy as jnp
from jax import lax
from jax.sharding import PartitionSpec as P


def on_device(dosage, snp_scale, covariates, previous, expression):
    highest = lax.Precision.HIGHEST
    decoded = dosage.astype(jnp.float32) * snp_scale[None, :]
    gram = jnp.dot(covariates.T, covariates, precision=highest)
    cross = jnp.dot(covariates.T, decoded, precision=highest)
    gram, cross = lax.psum((gram, cross), ("samp", "gene"))
    factor = jnp.linalg.cholesky(gram)
    coef = jax.scipy.linalg.cho_solve((factor, True), cross)
    resid = (decoded - jnp.dot(covariates, coef, precision=highest)).astype(jnp.bfloat16)
    piece = lax.all_gather(previous, "gene", axis=0, tiled=True)
    partial_scores = lax.dot_general(
        piece, expression, (((0,), (0,)), ((), ())), preferred_element_type=jnp.float32
    )
    x_sq = jnp.einsum("sp,sp->p", piece, piece, preferred_element_type=jnp.float32)
    scores, x_sq = (partial_scores, x_sq)
    y_sq = jnp.einsum("sg,sg->g", expression, expression, preferred_element_type=jnp.float32)
    samples = expression.shape[0] * lax.axis_size("samp")
    root = jnp.sqrt(jnp.float32(samples))
    shares, y_share = (
        lax.psum_scatter(scores, "samp", scatter_dimension=1, tiled=True),
        lax.psum_scatter(y_sq, "samp", scatter_dimension=0, tiled=True),
    )
    x_sq = lax.psum(x_sq, "samp")
    denom = jnp.sqrt(x_sq + 1e-06)[:, None] * jnp.sqrt(y_share + 1e-06)[None, :]
    z_part = (root * shares / denom).astype(jnp.bfloat16)
    zscores = lax.all_gather(z_part, "samp", axis=1, tiled=True)
    return (resid, zscores)


def solution(mesh):
    placed = (
        P(("samp", "gene"), "snp"),
        P("snp"),
        P(("samp", "gene"), None),
        P(("samp", "gene"), "snp"),
        P("samp", "gene"),
    )
    return jax.shard_map(
        on_device,
        mesh=mesh,
        in_specs=placed,
        out_specs=(P(("samp", "gene"), "snp"), P("snp", "gene")),
        check_vma=False,
    )
```

profile of v0, /device:TPU:0, one launch (start us, length us, event | category | flops | bytes accessed | tf_op | source)
XLA Modules:
  0.0 232.6 jit_solution(6112075205556040852)
XLA Ops:
  8.0 0.0 all-gather.3.cloned.1.call-start
  8.1 0.7 all-gather.3.cloned.1.call-update
  8.7 0.0 reduce-scatter.2.cloned.1.call-start
  8.8 40.4 %all-gather.3.cloned.1.call-done = bf16[4608,256]{1,0:T(8,128)(2,1)} async-done(((bf16[2304,256]{1,0:T(8,128)(2,1)}), bf16[4608,256]{1,0:T(8,128)(2,1)}) %all-gather.3.cloned.1.call-update) | async-done | bytes 2359312 | tf_op jit(solution)/shard_map/all_gather | solution.py:16
  49.2 39.2 %fusion.15 = f32[256,10240]{1,0:T(8,128)} fusion(bf16[4608,256]{1,0:T(8,128)(2,1)} %all-gather.3.cloned.1.call-done, bf16[4608,10240]{1,0:T(8,128)(2,1)} %param.9), kind=kOutput, calls=%fused_computation.28 | convolution fusion | flops 24159191040 | bytes 107216896 | tf_op jit(solution)/shard_map/dot_general | solution.py:17
  88.4 0.0 reduce-scatter.2.cloned.1.call-update
  88.4 0.0 all-reduce.4.cloned.1.call-start
  88.5 1.2 copy-done.1
  89.6 0.7 copy.11
  90.4 2.7 %fusion.6 = f32[64,256]{0,1:T(8,128)} fusion(f32[2304,64]{0,1:T(8,128)S(1)} %copy-done, bf16[2304,256]{0,1:T(8,128)(2,1)S(1)} %copy.11, f32[256]{0:T(256)S(1)} %copy-done.2), kind=kOutput, calls=%fused_computation.11 | convolution fusion | flops 454164480 | bytes 1836032 | tf_op jit(solution)/shard_map/dot_general | solution.py:11
  93.1 0.0 all-reduce.4.cloned.1.call-update
  93.1 0.0 all-gather.5.cloned.1.call-start
  93.2 35.1 %fusion = f32[10240]{0:T(1024)S(1)} fusion(bf16[4608,10240]{1,0:T(8,128)(2,1)} %param.9), kind=kLoop, calls=%fused_computation.1 | loop fusion | flops 141547520 | bytes 94412800 | tf_op jit(solution)/shard_map/sg,sg->g/dot_general | solution.py:22
  128.3 0.6 dynamic-slice
  129.5 2.4 %fusion.1 = f32[256]{0:T(256)S(1)} fusion(bf16[4608,256]{1,0:T(8,128)(2,1)} %all-gather.3.cloned.1.call-done), kind=kLoop, calls=%fused_computation.3 | loop fusion | flops 3538688 | bytes 2360320 | tf_op jit(solution)/shard_map/sp,sp->p/dot_general | solution.py:20
  131.9 13.8 %all-reduce.1 = (f32[10240]{0:T(1024)S(1)}, f32[256]{0:T(256)S(1)}) all-reduce(f32[10240]{0:T(1024)S(1)} %fusion, f32[256]{0:T(256)S(1)} %fusion.1), channel_id=3, replica_groups=mesh['samp'=4,'snp'=4,'gene'=2] {'samp'}, use_global_device_ids=true, to_apply=%region_6.7.clone | all-reduce | flops 10496 | bytes 83968
  145.7 0.1 fusion.13
  145.8 28.1 %reduce-scatter.2.cloned.1.call-done = f32[256,2560]{1,0:T(8,128)} async-done(((f32[256,10240]{1,0:T(8,128)}), f32[256,2560]{1,0:T(8,128)}) %reduce-scatter.2.cloned.1.call-update) | async-done | bytes 2621456 | tf_op jit(solution)/shard_map/reduce_scatter | solution.py:26
  173.9 3.3 %divide_convert_fusion = bf16[256,2560]{1,0:T(8,128)(2,1)} fusion(f32[256,2560]{1,0:T(8,128)} %reduce-scatter.2.cloned.1.call-done, f32[2560]{0:T(1024)S(1)} %fusion.13, f32[256]{0:T(256)S(1)} %add_sqrt_fusion), kind=kLoop, calls=%fused_computation.7 | loop fusion | flops 2621440 | bytes 3943424 | tf_op jit(solution)/shard_map/convert_element_type | solution.py:31
  177.2 0.6 fusion.14
  177.9 25.0 %psum.21 = f32[64,64]{0,1:T(8,128)S(1)} all-reduce(f32[64,64]{0,1:T(8,128)S(1)} %fusion.14), channel_id=1, replica_groups=mesh['samp'=4,'snp'=4,'gene'=2] {'samp','gene'}, use_global_device_ids=true, to_apply=%region_0.0 | all-reduce | flops 4096 | bytes 32768 | tf_op jit(solution)/shard_map/psum | solution.py:12
  202.9 0.1 copy.13
  203.0 5.8 %cholesky.16 = f32[64,64]{1,0:T(8,128)S(1)} custom-call(f32[64,64]{1,0:T(8,128)S(1)} %fusion.12), custom_call_target="Cholesky" | custom-call | tf_op jit(solution)/shard_map/jit(cholesky)/cholesky | solution.py:13
  208.9 0.7 compare_reduce_fusion
  209.5 0.6 fusion.7
  210.2 4.9 %custom-call.10 = f32[1,64,64]{1,2,0:T(8,128)S(1)} custom-call(f32[1,64,64]{2,1,0:T(8,128)S(1)} %fusion.7), custom_call_target="InvertDiagBlocksLowerTriangular" | custom-call | tf_op jit(solution)/shard_map/jit(_cho_solve)/triangular_solve | solution.py:14
  215.1 0.0 all-reduce.4.cloned.1.call-done
  215.1 1.2 fusion.10
  216.3 0.2 fusion.8
  216.5 2.1 fusion.3
  218.6 1.4 copy.14
  220.0 5.4 %copy.30 = bf16[256,10240]{1,0:T(8,128)(2,1)} copy(bf16[256,10240]{1,0:T(8,128)(2,1)} %all-gather.5.cloned.1.call-done) | data formatting | bytes 10485760
  (12 shorter events, 0.1 us)
Async XLA Ops:
  8.0 82.4 %copy-start = (f32[2304,64]{0,1:T(8,128)S(1)}, f32[2304,64]{0,1:T(8,128)}, u32[]{:S(2)}) copy-start(f32[2304,64]{0,1:T(8,128)} %param.7) | copy-start | bytes 1769476
  8.0 41.2 %all-gather.3.cloned.1.call-start = ((), (), s32[]{:S(2)}) async-start(), calls=%async_computation.2 | async-start | bytes 3538944 | tf_op jit(solution)/shard_map/all_gather | solution.py:16
  8.7 165.2 %reduce-scatter.2.cloned.1.call-start = ((), (), s32[]{:S(2)}) async-start(), calls=%async_computation.3 | async-start | bytes 13107200 | tf_op jit(solution)/shard_map/reduce_scatter | solution.py:26
  88.4 1.3 copy-start.1
  88.4 2.0 copy-start.2
  88.4 126.7 %all-reduce.4.cloned.1.call-start = ((), (), s32[]{:S(2)}) async-start(), calls=%async_computation.1 | async-start | bytes 262144 | tf_op jit(solution)/shard_map/psum | solution.py:12
  93.1 127.0 %all-gather.5.cloned.1.call-start = ((), (), s32[]{:S(2)}) async-start(), calls=%async_computation.4 | async-start | bytes 6553600 | tf_op jit(solution)/shard_map/all_gather | solution.py:32
  93.2 35.1 %copy-start.3 = (u32[32]{0:T(128)S(1)}, u32[32]{0:T(128)}, u32[]{:S(2)}) copy-start(u32[32]{0:T(128)} %constant.58) | copy-start | bytes 388
Sparse Core Ops, SparseCore 0:
  10.4 38.7 all-gather.2
  88.5 85.3 reduce-scatter.1
  177.4 40.6 all-gather.4
Sparse Core Ops, SparseCore 1:
  93.2 121.3 all-reduce.3
where the time goes:
time: 233 us
  waiting for transfers between devices  69.2 us (30%)
  other arithmetic  53 us (23%)
  matrix products  46 us (20%)
  blocking collectives  38.8 us (17%)
  between operations  16 us (7%)
  local copies, waits for them, and re-layouts  9.4 us (4%)
    all_gather x1, waiting for transfers between devices, on_device(): piece = lax.all_gather(previous, 'gene', axis=0, tiled=True)  40.4 us
    dot_general x1, matrix products, on_device(): lax.dot_general(piece, expression, (((0,), (0,)), ((), ())), preferred_el...  39.2 us
    dot_general x1, other arithmetic, on_device(): jnp.einsum('sg,sg->g', expression, expression, preferred_element_type=jnp...  35.1 us
    reduce_scatter x1, waiting for transfers between devices, on_device(): lax.psum_scatter(scores, 'samp', scatter_dimension=1, tiled=True)  28.1 us
    psum x1, blocking collectives, on_device(): gram, cross = lax.psum((gram, cross), ('samp', 'gene'))  25 us
    unnamed x1, blocking collectives  13.8 us
    unnamed x12, local copies, waits for them, and re-layouts  9.32 us
    another operation x3, other arithmetic, on_device(): factor = jnp.linalg.cholesky(gram)  6.55 us
  transfers between devices with their start and end apart: 4, of which 2 were waited for; matrix products, arithmetic and copies ran while one was open for 27% of the time, Pallas kernels for 0%

commit v1 on v0

v1 whole, which is shorter than its diff:
```python
import jax
import jax.numpy as jnp
from jax import lax
from jax.experimental import pallas as pl
from jax.experimental.pallas import tpu as pltpu
from jax.sharding import PartitionSpec as P


LANES = 128
SUBLANES = 8
LAG = 3
HIGHEST = lax.Precision.HIGHEST


def swap(value, axis, bit):
    count = lax.axis_size(axis)
    return lax.ppermute(value, axis, [(i, i ^ bit) for i in range(count)])


def after(*values):
    return lax.optimization_barrier(values)


def chunk_kernel(steps, squares, start, order_ref, mine_left, early_left, late_left, right_hbm, send_ref, pass_ref, mine_ref, acc_ref, right_ref, sems):
    half, rows, depth = mine_left.shape
    width = pass_ref.shape[1]

    def fetch(step):
        part = (step // half) ^ order_ref[4]
        row = pl.multiple_of((part * half + step % half) * depth, depth)
        return pltpu.make_async_copy(
            right_hbm.at[pl.ds(row, depth), pl.ds(start, 4 * width)], right_ref.at[step], sems.at[step]
        )

    for step in range(steps):
        fetch(step).start()
    acc_ref[...] = jnp.zeros_like(acc_ref)

    @pl.loop(0, steps)
    def _(step):
        other = jnp.where(step < half + half // 2, early_left[jnp.clip(step - half, 0, half // 2 - 1)], late_left[jnp.clip(step - half - half // 2, 0, half // 2 - 1)])
        left = jnp.where(step < half, mine_left[jnp.minimum(step, half - 1)], other)
        fetch(step).wait()
        right = right_ref[step]
        acc_ref[:rows] += jnp.dot(left, right, preferred_element_type=jnp.float32)
        if squares:
            wide = right.astype(jnp.float32)
            acc_ref[rows:] += jnp.sum((wide * wide).reshape(-1, SUBLANES, 4 * width), axis=0)

    def block(at):
        return acc_ref[:, pl.ds(pl.multiple_of(order_ref[at] * width, LANES), width)]

    send_ref[0] = block(0)
    send_ref[1] = block(1)
    pass_ref[...] = block(2)
    mine_ref[...] = block(3)


def chunk_products(order, lefts, right, start, width, squares):
    half, rows, depth = lefts[0].shape
    steps = 2 * half
    high = rows + (SUBLANES if squares else 0)
    shape = jax.ShapeDtypeStruct((high, width), jnp.float32)
    vmem = pl.BlockSpec(memory_space=pltpu.VMEM)
    return pl.pallas_call(
        lambda *refs: chunk_kernel(steps, squares, start, *refs),
        out_shape=(jax.ShapeDtypeStruct((2, high, width), jnp.float32), shape, shape),
        in_specs=[pl.BlockSpec(memory_space=pltpu.SMEM), vmem, vmem, vmem, pl.BlockSpec(memory_space=pl.ANY)],
        out_specs=(vmem, vmem, vmem),
        scratch_shapes=[
            pltpu.VMEM((high, 4 * width), jnp.float32),
            pltpu.VMEM((steps, depth, 4 * width), jnp.bfloat16),
            pltpu.SemaphoreType.DMA((steps,)),
        ],
        compiler_params=pltpu.CompilerParams(vmem_limit_bytes=36 << 20),
        cost_estimate=pl.CostEstimate(flops=1000, bytes_accessed=1000, transcendentals=0),
        name="chunk_products",
    )(order, *lefts, right)


def plan(genes):
    width = 4 * LANES
    count = genes // (4 * width) - 1
    out = [(c * 4 * width, width) for c in range(count)]
    return out + [(count * 4 * width, width // 2), (count * 4 * width + 2 * width, width // 2)]


def fast(dosage, snp_scale, covariates, previous, expression):
    samp, gene = lax.axis_index("samp"), lax.axis_index("gene")
    low, high = samp & 1, samp >> 1

    def owner(h, c):
        return 2 * h + c

    order = jnp.stack([owner(1 - high, 1 - low), owner(high, 1 - low), owner(1 - high, low), owner(high, low), gene]).astype(jnp.int32)
    local, snps = previous.shape
    deep, genes = expression.shape
    samples = deep * lax.axis_size("samp")
    split = 2
    depth = local // split

    def turned(block):
        return block.reshape(-1, depth, snps).transpose(0, 2, 1)

    first_rows, previous, covariates, dosage = after(previous[:depth], previous, covariates, dosage)
    other_a = swap(first_rows, "gene", 1)

    decoded = dosage.astype(jnp.float32) * snp_scale[None, :]
    covs = covariates.shape[1]
    gram = jnp.dot(covariates.T, covariates, precision=HIGHEST)
    cross = jnp.dot(covariates.T, decoded, precision=HIGHEST)
    wide = previous.astype(jnp.float32)
    x_own = jnp.sum(wide * wide, axis=0)
    top = jnp.concatenate([cross, jnp.pad(gram, ((0, 0), (0, -covs % LANES)))], axis=1)
    bottom = jnp.pad(x_own[None], ((0, SUBLANES - 1), (0, top.shape[1] - snps)))
    sums = jnp.concatenate([top, bottom], axis=0)
    sums, last_rows = after(sums, previous[depth:])
    sums_got = swap(sums, "gene", 1)
    other_b = swap(last_rows, "gene", 1)

    for bit in (1, 2):
        sums = sums + sums_got
        sums_got = swap(sums, "samp", bit)
    sums = sums + sums_got
    order, sums = after(order, sums)
    cross, gram = sums[:covs, :snps], sums[:covs, snps : snps + covs]
    x_root = jnp.sqrt(sums[covs, :snps] + 1e-06)[:, None]
    lefts = (turned(previous), turned(other_a), turned(other_b))
    root = jnp.sqrt(jnp.float32(samples))

    zscores = jnp.zeros((snps, genes), jnp.bfloat16)
    places = (owner(high, low), owner(1 - high, low), owner(high, 1 - low), owner(1 - high, 1 - low))
    work = plan(genes)
    onwards, z_owns, pending = [], [], []
    for at in range(len(work) + LAG):
        if at < len(work):
            start, width = work[at]
            if at >= 2:
                order, onwards[at - 2] = after(order, onwards[at - 2])
            if at >= LAG:
                order, z_owns[at - LAG] = after(order, z_owns[at - LAG])
            send, onward, mine = chunk_products(order, lefts, expression, start, width, True)
            got = swap(send, "samp", 1)
            onwards.append(onward + got[0])
            pending.append((mine, got))
        back = at - LAG + 1
        if 0 <= back < len(work):
            mine, got = pending[back]
            far = swap(onwards[back], "samp", 2)
            x_root, far = after(x_root, far)
            share = mine + got[1] + far
            y_root = jnp.sqrt(jnp.sum(share[snps:], axis=0) + 1e-06)[None, :]
            z_owns.append((root * share[:snps] / (x_root * y_root)).astype(jnp.bfloat16))
    gram, cross, onwards[-1] = after(gram, cross, onwards[-1])
    factor = jnp.linalg.cholesky(gram)
    coef = jax.scipy.linalg.cho_solve((factor, True), cross)
    resid = (decoded - jnp.dot(covariates, coef, precision=HIGHEST)).astype(jnp.bfloat16)
    resid, z_owns[-2] = after(resid, z_owns[-2])
    for at, (start, width) in enumerate(work):
        z_own = z_owns[at]
        z_far = swap(z_own, "samp", 2)
        pieces = (z_own, z_far, swap(z_own, "samp", 1), swap(z_far, "samp", 1))
        block = []
        for spot in range(4):
            value = pieces[3]
            for near in range(3):
                value = jnp.where(places[near] == spot, pieces[near], value)
            block.append(value)
        zscores = lax.dynamic_update_slice(zscores, jnp.concatenate(block, axis=1), (0, start))

    return (resid, zscores)


def general(dosage, snp_scale, covariates, previous, expression):
    decoded = dosage.astype(jnp.float32) * snp_scale[None, :]
    gram = jnp.dot(covariates.T, covariates, precision=HIGHEST)
    cross = jnp.dot(covariates.T, decoded, precision=HIGHEST)
    gram, cross = lax.psum((gram, cross), ("samp", "gene"))
    factor = jnp.linalg.cholesky(gram)
    coef = jax.scipy.linalg.cho_solve((factor, True), cross)
    resid = (decoded - jnp.dot(covariates, coef, precision=HIGHEST)).astype(jnp.bfloat16)
    piece = lax.all_gather(previous, "gene", axis=0, tiled=True)
    partial = lax.dot_general(
        piece, expression, (((0,), (0,)), ((), ())), preferred_element_type=jnp.float32
    )
    x_sq = jnp.einsum("sp,sp->p", piece, piece, preferred_element_type=jnp.float32)
    y_sq = jnp.einsum("sg,sg->g", expression, expression, preferred_element_type=jnp.float32)
    samples = expression.shape[0] * lax.axis_size("samp")
    root = jnp.sqrt(jnp.float32(samples))
    shares = lax.psum_scatter(partial, "samp", scatter_dimension=1, tiled=True)
    y_share = lax.psum_scatter(y_sq, "samp", scatter_dimension=0, tiled=True)
    x_sq = lax.psum(x_sq, "samp")
    denom = jnp.sqrt(x_sq + 1e-06)[:, None] * jnp.sqrt(y_share + 1e-06)[None, :]
    z_part = (root * shares / denom).astype(jnp.bfloat16)
    return (resid, lax.all_gather(z_part, "samp", axis=1, tiled=True))


def solution(mesh):
    placed = (
        P(("samp", "gene"), "snp"),
        P("snp"),
        P(("samp", "gene"), None),
        P(("samp", "gene"), "snp"),
        P("samp", "gene"),
    )

    def on_device(*args):
        genes, snps = args[4].shape[1], args[3].shape[1]
        fits = mesh.shape["samp"] == 4 and mesh.shape["gene"] == 2
        fits = fits and genes % (16 * LANES) == 0 and genes >= 48 * LANES and snps % LANES == 0 and args[3].shape[0] % (2 * LANES) == 0
        return fast(*args) if fits else general(*args)

    return jax.shard_map(
        on_device,
        mesh=mesh,
        in_specs=placed,
        out_specs=(P(("samp", "gene"), "snp"), P("snp", "gene")),
        check_vma=False,
    )
```

time: 233 us -> 193 us (0.83)
  Pallas kernels: 0 us -> 53.7 us
  blocking collectives: 38.8 us -> 0 us
  matrix products: 46 us -> 8.02 us
  starting transfers between devices: 0.16 us -> 24.8 us
  other arithmetic: 53 us -> 32.1 us
  between operations: 16 us -> 1.19 us
  waiting for transfers between devices: 69.2 us -> 61.8 us
    ppermute x0 -> x35, waiting for transfers between devices: none -> 61.8 us  [swap(): return lax.ppermute(value, axis, [(i, i ^ bit) for i in range(count)])]
    pallas_call x0 -> x6, Pallas kernels: none -> 53.7 us  [chunk_products(): pl.pallas_call(lambda *refs: chunk_kernel(steps, squares, start, *refs),...]
    all_gather x2 -> x0, waiting for transfers between devices: 40.4 us -> none  [the longest x1 40.4 us: on_device(): piece = lax.all_gather(previous, 'gene', axis=0, tiled=True)]
    dot_general x2 -> x0, other arithmetic: 37.5 us -> none  [the longest x1 35.1 us: on_device(): jnp.einsum('sg,sg->g', expression, expression, preferred_element_type=jnp...]
    dot_general x4 -> x3, matrix products: 44.6 us -> 7.53 us  [the longest x1 3.82 us: fast(): cross = jnp.dot(covariates.T, decoded, precision=HIGHEST)]
    reduce_scatter x1 -> x0, waiting for transfers between devices: 28.1 us -> none  [on_device(): lax.psum_scatter(scores, 'samp', scatter_dimension=1, tiled=True)]
    psum x1 -> x0, blocking collectives: 25 us -> none  [on_device(): gram, cross = lax.psum((gram, cross), ('samp', 'gene'))]
    ppermute x0 -> x35, starting transfers between devices: none -> 24.8 us  [swap(): return lax.ppermute(value, axis, [(i, i ^ bit) for i in range(count)])]
  transfers between devices with their start and end apart: 4 -> 35, of which waited for: 2 -> 9; matrix products, arithmetic and copies ran while one was open for 27% -> 24% of each run, Pallas kernels for 0% -> 23%
where the time goes in v1:
time: 193 us
  waiting for transfers between devices  61.8 us (32%)
  Pallas kernels  53.7 us (28%)
  other arithmetic  32.1 us (17%)
  starting transfers between devices  24.8 us (13%)
  local copies, waits for them, and re-layouts  11.2 us (6%)
  matrix products  8.02 us (4%)
    ppermute x35, waiting for transfers between devices, swap(): return lax.ppermute(value, axis, [(i, i ^ bit) for i in range(count)])  61.8 us
    pallas_call x6, Pallas kernels, chunk_products(): pl.pallas_call(lambda *refs: chunk_kernel(steps, squares, start, *refs),...  53.7 us
    ppermute x35, starting transfers between devices, swap(): return lax.ppermute(value, axis, [(i, i ^ bit) for i in range(count)])  24.8 us
    another operation x3, other arithmetic, fast(): factor = jnp.linalg.cholesky(gram)  6.53 us
    another operation x2, other arithmetic, fast(): coef = jax.scipy.linalg.cho_solve((factor, True), cross)  5.53 us
    add x6, other arithmetic, fast(): share = mine + got[1] + far  4.8 us
    dynamic_update_slice x5, other arithmetic, fast(): lax.dynamic_update_slice(zscores, jnp.concatenate(block, axis=1), (0, sta...  4.05 us
    add x6, other arithmetic, fast(): onwards.append(onward + got[0])  3.98 us
  transfers between devices with their start and end apart: 35, of which 9 were waited for; matrix products, arithmetic and copies ran while one was open for 24% of the time, Pallas kernels for 23%

profile of v1, /device:TPU:0, one launch (start us, length us, event | category | flops | bytes accessed | tf_op | source)
XLA Modules:
  0.0 192.7 jit_solution(17793047518763446110)
XLA Ops:
  2.9 3.0 %collective-permute-start.3 = (bf16[1152,256]{0,1:T(8,128)(2,1)}, bf16[1152,256]{0,1:T(8,128)(2,1)S(1)}, u32[]{:S(2)}, u32[]{:S(2)}) collective-permute-start(bf16[1152,256]{0,1:T(8,128)(2,1)} %copy.28), channel_id=1, source_target_pairs={{0,1},{1,0},{2,3},{3,2},{4,5},{5,4},{6,7},{7,6},{8,9},{9,8},{10,11... | collective-permute-start | bytes 1769480 | tf_op jit(solution)/shard_map/ppermute | solution.py:17
  6.3 1.5 copy.23
  8.6 1.9 slice.134
  10.5 3.8 %fusion.8 = f32[64,256]{0,1:T(8,128)S(1)} fusion(f32[2304,64]{0,1:T(8,128)S(1)} %copy-done, bf16[2304,256]{1,0:T(8,128)(2,1)S(1)} %copy-done.7, f32[256]{0:T(256)S(1)} %copy-done.18), kind=kOutput, calls=%fused_computation.12 | convolution fusion | flops 454164480 | bytes 1836032 | tf_op jit(solution)/shard_map/dot_general | solution.py:111
  14.5 2.0 %collective-permute-start = (f32[72,384]{0,1:T(8,128)S(1)}, f32[72,384]{0,1:T(8,128)S(1)}, u32[]{:S(2)}, u32[]{:S(2)}) collective-permute-start(f32[72,384]{0,1:T(8,128)S(1)} %select_maximum_fusion), channel_id=1, source_target_pairs={{0,1},{1,0},{2,3},{3,2},{4,5},{5,4},{6,7},{7,6},{8,9},{9,8},{10,11... | collective-permute-start | bytes 331784 | tf_op jit(solution)/shard_map/ppermute | solution.py:17
  16.5 19.8 %collective-permute-done = f32[72,384]{0,1:T(8,128)S(1)} collective-permute-done((f32[72,384]{0,1:T(8,128)S(1)}, f32[72,384]{0,1:T(8,128)S(1)}, u32[]{:S(2)}, u32[]{:S(2)}) %collective-permute-start) | collective-permute-done | bytes 110624 | tf_op jit(solution)/shard_map/ppermute | solution.py:17
  37.9 1.8 collective-permute-start.2
  39.7 1.7 copy.24
  41.4 3.5 %collective-permute-done.2 = f32[72,384]{0,1:T(8,128)S(1)} collective-permute-done((f32[72,384]{0,1:T(8,128)S(1)}, f32[72,384]{0,1:T(8,128)S(1)}, u32[]{:S(2)}, u32[]{:S(2)}) %collective-permute-start.2) | collective-permute-done | bytes 110624 | tf_op jit(solution)/shard_map/ppermute | solution.py:17
  45.6 9.6 %chunk_products.6 = (f32[2,264,512]{2,1,0:T(8,128)S(1)}, f32[264,512]{1,0:T(8,128)S(1)}, f32[264,512]{1,0:T(8,128)S(1)}) custom-call(s32[5]{0:T(128)S(1)} %stack.23.refs_0_, bf16[2,256,1152]{2,1,0:T(8,128)(2,1)S(1)} %bitcast.99, bf16[1,256,1152]{2,1,0:T(8,128)(2,1)S(1)} %bitcast.105, bf16[1,256,1152]{2,1,0:T(8,128)(2,1)S(1)} %bitcast.111, ...), custom_call_target="tpu_custom_call" | custom-call | flops 1000 | bytes 1000 | tf_op jit(solution)/shard_map/chunk_products/pallas_call | solution.py:65
  56.1 10.6 %chunk_products.7 = (f32[2,264,512]{2,1,0:T(8,128)}, f32[264,512]{1,0:T(8,128)S(1)}, f32[264,512]{1,0:T(8,128)S(1)}) custom-call(s32[5]{0:T(128)S(1)} %stack.23.refs_0_, bf16[2,256,1152]{2,1,0:T(8,128)(2,1)S(1)} %bitcast.100, bf16[1,256,1152]{2,1,0:T(8,128)(2,1)S(1)} %bitcast.106, bf16[1,256,1152]{2,1,0:T(8,128)(2,1)S(1)} %bitcast.112, ...), custom_call_target="tpu_custom_call" | custom-call | flops 1000 | bytes 1000 | tf_op jit(solution)/shard_map/chunk_products/pallas_call | solution.py:65
  68.4 1.7 collective-permute-start.7
  70.9 1.6 slice.108
  73.6 9.8 %chunk_products.8 = (f32[2,264,512]{2,1,0:T(8,128)S(1)}, f32[264,512]{1,0:T(8,128)S(1)}, f32[264,512]{1,0:T(8,128)S(1)}) custom-call(s32[5]{0:T(128)S(1)} %stack.23.refs_0_, bf16[2,256,1152]{2,1,0:T(8,128)(2,1)S(1)} %bitcast.101, bf16[1,256,1152]{2,1,0:T(8,128)(2,1)S(1)} %bitcast.107, bf16[1,256,1152]{2,1,0:T(8,128)(2,1)S(1)} %bitcast.113, ...), custom_call_target="tpu_custom_call" | custom-call | flops 1000 | bytes 1000 | tf_op jit(solution)/shard_map/chunk_products/pallas_call | solution.py:65
  86.4 1.8 collective-permute-start.17
  88.4 11.4 %collective-permute-done.9 = f32[264,512]{1,0:T(8,128)S(1)} collective-permute-done((f32[264,512]{1,0:T(8,128)S(1)}, f32[264,512]{1,0:T(8,128)S(1)}, u32[]{:S(2)}, u32[]{:S(2)}) %collective-permute-start.9) | collective-permute-done | bytes 540704 | tf_op jit(solution)/shard_map/ppermute | solution.py:17
  101.0 3.2 %collective-permute-done.17 = bf16[256,512]{1,0:T(8,128)(2,1)S(1)} collective-permute-done((bf16[256,512]{1,0:T(8,128)(2,1)S(1)}, bf16[256,512]{1,0:T(8,128)(2,1)S(1)}, u32[]{:S(2)}, u32[]{:S(2)}) %collective-permute-start.17) | collective-permute-done | bytes 262176 | tf_op jit(solution)/shard_map/ppermute | solution.py:17
  104.3 9.6 %chunk_products.9 = (f32[2,264,512]{2,1,0:T(8,128)S(1)}, f32[264,512]{1,0:T(8,128)S(1)}, f32[264,512]{1,0:T(8,128)S(1)}) custom-call(s32[5]{0:T(128)S(1)} %stack.23.refs_0_, bf16[2,256,1152]{2,1,0:T(8,128)(2,1)S(1)} %bitcast.102, bf16[1,256,1152]{2,1,0:T(8,128)(2,1)S(1)} %bitcast.108, bf16[1,256,1152]{2,1,0:T(8,128)(2,1)S(1)} %bitcast.114, ...), custom_call_target="tpu_custom_call" | custom-call | flops 1000 | bytes 1000 | tf_op jit(solution)/shard_map/chunk_products/pallas_call | solution.py:65
  115.3 1.7 collective-permute-start.11
  117.6 6.2 %chunk_products.11 = (f32[2,264,256]{2,1,0:T(8,128)S(1)}, f32[264,256]{1,0:T(8,128)S(1)}, f32[264,256]{1,0:T(8,128)S(1)}) custom-call(s32[5]{0:T(128)S(1)} %stack.23.refs_0_, bf16[2,256,1152]{2,1,0:T(8,128)(2,1)S(1)} %bitcast.103, bf16[1,256,1152]{2,1,0:T(8,128)(2,1)S(1)} %bitcast.109, bf16[1,256,1152]{2,1,0:T(8,128)(2,1)S(1)} %bitcast.115, ...), custom_call_target="tpu_custom_call" | custom-call | flops 1000 | bytes 1000 | tf_op jit(solution)/shard_map/chunk_products/pallas_call | solution.py:65
  124.5 10.3 %collective-permute-done.11 = f32[264,512]{1,0:T(8,128)S(1)} collective-permute-done((f32[264,512]{1,0:T(8,128)S(1)}, f32[264,512]{1,0:T(8,128)S(1)}, u32[]{:S(2)}, u32[]{:S(2)}) %collective-permute-start.11) | collective-permute-done | bytes 540704 | tf_op jit(solution)/shard_map/ppermute | solution.py:17
  135.9 1.8 collective-permute-start.14
  137.6 6.9 %collective-permute-done.23 = bf16[256,512]{1,0:T(8,128)(2,1)S(1)} collective-permute-done((bf16[256,512]{1,0:T(8,128)(2,1)S(1)}, bf16[256,512]{1,0:T(8,128)(2,1)S(1)}, u32[]{:S(2)}, u32[]{:S(2)}) %collective-permute-start.23) | collective-permute-done | bytes 262176 | tf_op jit(solution)/shard_map/ppermute | solution.py:17
  144.7 7.7 %chunk_products.10 = (f32[2,264,256]{2,1,0:T(8,128)S(1)}, f32[264,256]{1,0:T(8,128)S(1)}, f32[264,256]{1,0:T(8,128)S(1)}) custom-call(s32[5]{0:T(128)S(1)} %stack.23.refs_0_, bf16[2,256,1152]{2,1,0:T(8,128)(2,1)S(1)} %bitcast.104, bf16[1,256,1152]{2,1,0:T(8,128)(2,1)S(1)} %bitcast.110, bf16[1,256,1152]{2,1,0:T(8,128)(2,1)S(1)} %bitcast.116, ...), custom_call_target="tpu_custom_call" | custom-call | flops 1000 | bytes 1000 | tf_op jit(solution)/shard_map/chunk_products/pallas_call | solution.py:65
  156.2 1.7 collective-permute-start.26
  159.2 5.8 %cholesky.16 = f32[64,64]{1,0:T(8,128)S(1)} custom-call(f32[64,64]{1,0:T(8,128)S(1)} %fusion.46), custom_call_target="Cholesky" | custom-call | tf_op jit(solution)/shard_map/jit(cholesky)/cholesky | solution.py:155
  166.4 4.9 %custom-call.10 = f32[1,64,64]{1,2,0:T(8,128)S(1)} custom-call(f32[1,64,64]{2,1,0:T(8,128)S(1)} %fusion.41), custom_call_target="InvertDiagBlocksLowerTriangular" | custom-call | tf_op jit(solution)/shard_map/jit(_cho_solve)/triangular_solve | solution.py:156
  173.0 3.1 %fusion.7 = bf16[2304,256]{1,0:T(8,128)(2,1)} fusion(f32[2304,64]{0,1:T(8,128)S(1)} %copy-done, f32[64,256]{1,0:T(8,128)S(1)} %fusion.42, bf16[2304,256]{1,0:T(8,128)(2,1)S(1)} %copy-done.8, f32[256]{0:T(256)S(1)} %copy-done.19), kind=kOutput, calls=%fused_computation.9 | convolution fusion | flops 455344128 | bytes 3015680 | tf_op jit(solution)/shard_map/dot_general | solution.py:157
  176.2 1.8 collective-permute-start.29
  179.6 1.6 collective-permute-done.29
  182.9 1.8 collective-permute-start.33
  184.9 3.5 %collective-permute-done.33 = bf16[256,256]{1,0:T(8,128)(2,1)S(1)} collective-permute-done((bf16[256,256]{1,0:T(8,128)(2,1)S(1)}, bf16[256,256]{1,0:T(8,128)(2,1)S(1)}, u32[]{:S(2)}, u32[]{:S(2)}) %collective-permute-start.33) | collective-permute-done | bytes 131104 | tf_op jit(solution)/shard_map/ppermute | solution.py:17
  (153 shorter events, 34.1 us)
Async XLA Ops:
  2.9 42.6 %collective-permute-start.3 = (bf16[1152,256]{0,1:T(8,128)(2,1)}, bf16[1152,256]{0,1:T(8,128)(2,1)S(1)}, u32[]{:S(2)}, u32[]{:S(2)}) collective-permute-start(bf16[1152,256]{0,1:T(8,128)(2,1)} %copy.28), channel_id=1, source_target_pairs={{0,1},{1,0},{2,3},{3,2},{4,5},{5,4},{6,7},{7,6},{8,9},{9,8},{10,11... | collective-permute-start | bytes 1769480 | tf_op jit(solution)/shard_map/ppermute | solution.py:17
  14.5 31.1 %collective-permute-start.4 = (bf16[1152,256]{0,1:T(8,128)(2,1)}, bf16[1152,256]{0,1:T(8,128)(2,1)S(1)}, u32[]{:S(2)}, u32[]{:S(2)}) collective-permute-start(bf16[1152,256]{0,1:T(8,128)(2,1)} %slice.134), channel_id=1, source_target_pairs={{0,1},{1,0},{2,3},{3,2},{4,5},{5,4},{6,7},{7,6},{8,9},{9,8},{10,11... | collective-permute-start | bytes 1769480 | tf_op jit(solution)/shard_map/ppermute | solution.py:17
  14.5 21.8 %collective-permute-start = (f32[72,384]{0,1:T(8,128)S(1)}, f32[72,384]{0,1:T(8,128)S(1)}, u32[]{:S(2)}, u32[]{:S(2)}) collective-permute-start(f32[72,384]{0,1:T(8,128)S(1)} %select_maximum_fusion), channel_id=1, source_target_pairs={{0,1},{1,0},{2,3},{3,2},{4,5},{5,4},{6,7},{7,6},{8,9},{9,8},{10,11... | collective-permute-start | bytes 331784 | tf_op jit(solution)/shard_map/ppermute | solution.py:17
  37.9 7.0 %collective-permute-start.2 = (f32[72,384]{0,1:T(8,128)S(1)}, f32[72,384]{0,1:T(8,128)S(1)}, u32[]{:S(2)}, u32[]{:S(2)}) collective-permute-start(f32[72,384]{0,1:T(8,128)S(1)} %add.157), channel_id=1, source_target_pairs={{0,16},{8,24},{16,0},{24,8},{1,17},{9,25},{17,1},{25,9},{2,18},{10... | collective-permute-start | bytes 331784 | tf_op jit(solution)/shard_map/ppermute | solution.py:17
  56.1 11.2 %collective-permute-start.5 = (f32[2,264,512]{2,1,0:T(8,128)S(1)}, f32[2,264,512]{2,1,0:T(8,128)S(1)}, u32[]{:S(2)}, u32[]{:S(2)}) collective-permute-start(f32[2,264,512]{2,1,0:T(8,128)S(1)} %get-tuple-element.67), channel_id=1, source_target_pairs={{0,8},{8,0},{16,24},{24,16},{1,9},{9,1},{17,25},{25,17},{2,10},{10... | collective-permute-start | bytes 3244040 | tf_op jit(solution)/shard_map/ppermute | solution.py:17
  66.7 16.7 %collective-permute-start.6 = (f32[2,264,512]{2,1,0:T(8,128)}, f32[2,264,512]{2,1,0:T(8,128)}, u32[]{:S(2)}, u32[]{:S(2)}) collective-permute-start(f32[2,264,512]{2,1,0:T(8,128)} %get-tuple-element.70), channel_id=1, source_target_pairs={{0,8},{8,0},{16,24},{24,16},{1,9},{9,1},{17,25},{25,17},{2,10},{10... | collective-permute-start | bytes 3244040 | tf_op jit(solution)/shard_map/ppermute | solution.py:17
  68.4 16.6 %collective-permute-start.7 = (f32[264,512]{1,0:T(8,128)}, f32[264,512]{1,0:T(8,128)}, u32[]{:S(2)}, u32[]{:S(2)}) collective-permute-start(f32[264,512]{1,0:T(8,128)} %fusion.21), channel_id=1, source_target_pairs={{0,16},{8,24},{16,0},{24,8},{1,17},{9,25},{17,1},{25,9},{2,18},{10... | collective-permute-start | bytes 1622024 | tf_op jit(solution)/shard_map/ppermute | solution.py:17
  84.6 15.2 %collective-permute-start.9 = (f32[264,512]{1,0:T(8,128)S(1)}, f32[264,512]{1,0:T(8,128)S(1)}, u32[]{:S(2)}, u32[]{:S(2)}) collective-permute-start(f32[264,512]{1,0:T(8,128)S(1)} %fusion.20), channel_id=1, source_target_pairs={{0,16},{8,24},{16,0},{24,8},{1,17},{9,25},{17,1},{25,9},{2,18},{10... | collective-permute-start | bytes 1622024 | tf_op jit(solution)/shard_map/ppermute | solution.py:17
  85.0 29.9 %collective-permute-start.8 = (f32[2,264,512]{2,1,0:T(8,128)S(1)}, f32[2,264,512]{2,1,0:T(8,128)S(1)}, u32[]{:S(2)}, u32[]{:S(2)}) collective-permute-start(f32[2,264,512]{2,1,0:T(8,128)S(1)} %get-tuple-element.78), channel_id=1, source_target_pairs={{0,8},{8,0},{16,24},{24,16},{1,9},{9,1},{17,25},{25,17},{2,10},{10... | collective-permute-start | bytes 3244040 | tf_op jit(solution)/shard_map/ppermute | solution.py:17
  86.4 17.9 %collective-permute-start.17 = (bf16[256,512]{1,0:T(8,128)(2,1)S(1)}, bf16[256,512]{1,0:T(8,128)(2,1)S(1)}, u32[]{:S(2)}, u32[]{:S(2)}) collective-permute-start(bf16[256,512]{1,0:T(8,128)(2,1)S(1)} %fusion.29), channel_id=1, source_target_pairs={{0,16},{8,24},{16,0},{24,8},{1,17},{9,25},{17,1},{25,9},{2,18},{10... | collective-permute-start | bytes 786440 | tf_op jit(solution)/shard_map/ppermute | solution.py:17
  88.2 26.5 %collective-permute-start.16 = (bf16[256,512]{1,0:T(8,128)(2,1)S(1)}, bf16[256,512]{1,0:T(8,128)(2,1)S(1)}, u32[]{:S(2)}, u32[]{:S(2)}) collective-permute-start(bf16[256,512]{1,0:T(8,128)(2,1)S(1)} %fusion.29), channel_id=1, source_target_pairs={{0,8},{8,0},{16,24},{24,16},{1,9},{9,1},{17,25},{25,17},{2,10},{10... | collective-permute-start | bytes 786440 | tf_op jit(solution)/shard_map/ppermute | solution.py:17
  104.3 10.4 %collective-permute-start.18 = (bf16[256,512]{1,0:T(8,128)(2,1)S(1)}, bf16[256,512]{1,0:T(8,128)(2,1)S(1)}, u32[]{:S(2)}, u32[]{:S(2)}) collective-permute-start(bf16[256,512]{1,0:T(8,128)(2,1)S(1)} %collective-permute-done.17), channel_id=1, source_target_pairs={{0,8},{8,0},{16,24},{24,16},{1,9},{9,1},{17,25},{25,17},{2,10},{10... | collective-permute-start | bytes 786440 | tf_op jit(solution)/shard_map/ppermute | solution.py:17
  113.9 21.1 %collective-permute-start.10 = (f32[2,264,512]{2,1,0:T(8,128)S(1)}, f32[2,264,512]{2,1,0:T(8,128)S(1)}, u32[]{:S(2)}, u32[]{:S(2)}) collective-permute-start(f32[2,264,512]{2,1,0:T(8,128)S(1)} %get-tuple-element.86), channel_id=1, source_target_pairs={{0,8},{8,0},{16,24},{24,16},{1,9},{9,1},{17,25},{25,17},{2,10},{10... | collective-permute-start | bytes 3244040 | tf_op jit(solution)/shard_map/ppermute | solution.py:17
  114.9 9.5 %collective-permute-start.20 = (bf16[256,512]{1,0:T(8,128)(2,1)S(1)}, bf16[256,512]{1,0:T(8,128)(2,1)S(1)}, u32[]{:S(2)}, u32[]{:S(2)}) collective-permute-start(bf16[256,512]{1,0:T(8,128)(2,1)S(1)} %fusion.27), channel_id=1, source_target_pairs={{0,16},{8,24},{16,0},{24,8},{1,17},{9,25},{17,1},{25,9},{2,18},{10... | collective-permute-start | bytes 786440 | tf_op jit(solution)/shard_map/ppermute | solution.py:17
  115.3 19.5 %collective-permute-start.11 = (f32[264,512]{1,0:T(8,128)S(1)}, f32[264,512]{1,0:T(8,128)S(1)}, u32[]{:S(2)}, u32[]{:S(2)}) collective-permute-start(f32[264,512]{1,0:T(8,128)S(1)} %fusion.17), channel_id=1, source_target_pairs={{0,16},{8,24},{16,0},{24,8},{1,17},{9,25},{17,1},{25,9},{2,18},{10... | collective-permute-start | bytes 1622024 | tf_op jit(solution)/shard_map/ppermute | solution.py:17
  117.5 18.1 %collective-permute-start.19 = (bf16[256,512]{1,0:T(8,128)(2,1)S(1)}, bf16[256,512]{1,0:T(8,128)(2,1)S(1)}, u32[]{:S(2)}, u32[]{:S(2)}) collective-permute-start(bf16[256,512]{1,0:T(8,128)(2,1)S(1)} %fusion.27), channel_id=1, source_target_pairs={{0,8},{8,0},{16,24},{24,16},{1,9},{9,1},{17,25},{25,17},{2,10},{10... | collective-permute-start | bytes 786440 | tf_op jit(solution)/shard_map/ppermute | solution.py:17
  123.9 29.1 %collective-permute-start.13 = (f32[2,264,256]{2,1,0:T(8,128)S(1)}, f32[2,264,256]{2,1,0:T(8,128)S(1)}, u32[]{:S(2)}, u32[]{:S(2)}) collective-permute-start(f32[2,264,256]{2,1,0:T(8,128)S(1)} %get-tuple-element.98), channel_id=1, source_target_pairs={{0,8},{8,0},{16,24},{24,16},{1,9},{9,1},{17,25},{25,17},{2,10},{10... | collective-permute-start | bytes 1622024 | tf_op jit(solution)/shard_map/ppermute | solution.py:17
  124.4 11.2 %collective-permute-start.21 = (bf16[256,512]{1,0:T(8,128)(2,1)S(1)}, bf16[256,512]{1,0:T(8,128)(2,1)S(1)}, u32[]{:S(2)}, u32[]{:S(2)}) collective-permute-start(bf16[256,512]{1,0:T(8,128)(2,1)S(1)} %collective-permute-done.20), channel_id=1, source_target_pairs={{0,8},{8,0},{16,24},{24,16},{1,9},{9,1},{17,25},{25,17},{2,10},{10... | collective-permute-start | bytes 786440 | tf_op jit(solution)/shard_map/ppermute | solution.py:17
  135.3 9.2 %collective-permute-start.23 = (bf16[256,512]{1,0:T(8,128)(2,1)S(1)}, bf16[256,512]{1,0:T(8,128)(2,1)S(1)}, u32[]{:S(2)}, u32[]{:S(2)}) collective-permute-start(bf16[256,512]{1,0:T(8,128)(2,1)S(1)} %fusion.25), channel_id=1, source_target_pairs={{0,16},{8,24},{16,0},{24,8},{1,17},{9,25},{17,1},{25,9},{2,18},{10... | collective-permute-start | bytes 786440 | tf_op jit(solution)/shard_map/ppermute | solution.py:17
  135.8 18.4 %collective-permute-start.22 = (bf16[256,512]{1,0:T(8,128)(2,1)S(1)}, bf16[256,512]{1,0:T(8,128)(2,1)S(1)}, u32[]{:S(2)}, u32[]{:S(2)}) collective-permute-start(bf16[256,512]{1,0:T(8,128)(2,1)S(1)} %fusion.25), channel_id=1, source_target_pairs={{0,8},{8,0},{16,24},{24,16},{1,9},{9,1},{17,25},{25,17},{2,10},{10... | collective-permute-start | bytes 786440 | tf_op jit(solution)/shard_map/ppermute | solution.py:17
  135.9 19.3 %collective-permute-start.14 = (f32[264,512]{1,0:T(8,128)S(1)}, f32[264,512]{1,0:T(8,128)S(1)}, u32[]{:S(2)}, u32[]{:S(2)}) collective-permute-start(f32[264,512]{1,0:T(8,128)S(1)} %fusion.14), channel_id=1, source_target_pairs={{0,16},{8,24},{16,0},{24,8},{1,17},{9,25},{17,1},{25,9},{2,18},{10... | collective-permute-start | bytes 1622024 | tf_op jit(solution)/shard_map/ppermute | solution.py:17
  144.5 9.6 %collective-permute-start.24 = (bf16[256,512]{1,0:T(8,128)(2,1)S(1)}, bf16[256,512]{1,0:T(8,128)(2,1)S(1)}, u32[]{:S(2)}, u32[]{:S(2)}) collective-permute-start(bf16[256,512]{1,0:T(8,128)(2,1)S(1)} %collective-permute-done.23), channel_id=1, source_target_pairs={{0,8},{8,0},{16,24},{24,16},{1,9},{9,1},{17,25},{25,17},{2,10},{10... | collective-permute-start | bytes 786440 | tf_op jit(solution)/shard_map/ppermute | solution.py:17
  152.4 5.5 %collective-permute-start.12 = (f32[2,264,256]{2,1,0:T(8,128)S(1)}, f32[2,264,256]{2,1,0:T(8,128)S(1)}, u32[]{:S(2)}, u32[]{:S(2)}) collective-permute-start(f32[2,264,256]{2,1,0:T(8,128)S(1)} %get-tuple-element.94), channel_id=1, source_target_pairs={{0,8},{8,0},{16,24},{24,16},{1,9},{9,1},{17,25},{25,17},{2,10},{10... | collective-permute-start | bytes 1622024 | tf_op jit(solution)/shard_map/ppermute | solution.py:17
  153.8 18.0 %collective-permute-start.15 = (f32[264,256]{1,0:T(8,128)}, f32[264,256]{1,0:T(8,128)}, u32[]{:S(2)}, u32[]{:S(2)}) collective-permute-start(f32[264,256]{1,0:T(8,128)} %fusion.32), channel_id=1, source_target_pairs={{0,16},{8,24},{16,0},{24,8},{1,17},{9,25},{17,1},{25,9},{2,18},{10... | collective-permute-start | bytes 811016 | tf_op jit(solution)/shard_map/ppermute | solution.py:17
  156.2 25.1 %collective-permute-start.26 = (bf16[256,512]{1,0:T(8,128)(2,1)}, bf16[256,512]{1,0:T(8,128)(2,1)}, u32[]{:S(2)}, u32[]{:S(2)}) collective-permute-start(bf16[256,512]{1,0:T(8,128)(2,1)} %fusion.23), channel_id=1, source_target_pairs={{0,16},{8,24},{16,0},{24,8},{1,17},{9,25},{17,1},{25,9},{2,18},{10... | collective-permute-start | bytes 786440 | tf_op jit(solution)/shard_map/ppermute | solution.py:17
  158.8 22.9 %collective-permute-start.31 = (f32[264,256]{1,0:T(8,128)}, f32[264,256]{1,0:T(8,128)}, u32[]{:S(2)}, u32[]{:S(2)}) collective-permute-start(f32[264,256]{1,0:T(8,128)} %fusion.35), channel_id=1, source_target_pairs={{0,16},{8,24},{16,0},{24,8},{1,17},{9,25},{17,1},{25,9},{2,18},{10... | collective-permute-start | bytes 811016 | tf_op jit(solution)/shard_map/ppermute | solution.py:17
  176.2 5.0 %collective-permute-start.29 = (bf16[256,256]{1,0:T(8,128)(2,1)S(1)}, bf16[256,256]{1,0:T(8,128)(2,1)S(1)}, u32[]{:S(2)}, u32[]{:S(2)}) collective-permute-start(bf16[256,256]{1,0:T(8,128)(2,1)S(1)} %fusion.39), channel_id=1, source_target_pairs={{0,16},{8,24},{16,0},{24,8},{1,17},{9,25},{17,1},{25,9},{2,18},{10... | collective-permute-start | bytes 393224 | tf_op jit(solution)/shard_map/ppermute | solution.py:17
  179.1 9.3 %collective-permute-start.25 = (bf16[256,512]{1,0:T(8,128)(2,1)}, bf16[256,512]{1,0:T(8,128)(2,1)S(1)}, u32[]{:S(2)}, u32[]{:S(2)}) collective-permute-start(bf16[256,512]{1,0:T(8,128)(2,1)} %fusion.23), channel_id=1, source_target_pairs={{0,8},{8,0},{16,24},{24,16},{1,9},{9,1},{17,25},{25,17},{2,10},{10... | collective-permute-start | bytes 786440 | tf_op jit(solution)/shard_map/ppermute | solution.py:17
  179.1 5.6 %collective-permute-start.28 = (bf16[256,256]{1,0:T(8,128)(2,1)S(1)}, bf16[256,256]{1,0:T(8,128)(2,1)S(1)}, u32[]{:S(2)}, u32[]{:S(2)}) collective-permute-start(bf16[256,256]{1,0:T(8,128)(2,1)S(1)} %fusion.39), channel_id=1, source_target_pairs={{0,8},{8,0},{16,24},{24,16},{1,9},{9,1},{17,25},{25,17},{2,10},{10... | collective-permute-start | bytes 393224 | tf_op jit(solution)/shard_map/ppermute | solution.py:17
  181.3 7.2 %collective-permute-start.27 = (bf16[256,512]{1,0:T(8,128)(2,1)}, bf16[256,512]{1,0:T(8,128)(2,1)S(1)}, u32[]{:S(2)}, u32[]{:S(2)}) collective-permute-start(bf16[256,512]{1,0:T(8,128)(2,1)} %collective-permute-done.26), channel_id=1, source_target_pairs={{0,8},{8,0},{16,24},{24,16},{1,9},{9,1},{17,25},{25,17},{2,10},{10... | collective-permute-start | bytes 786440 | tf_op jit(solution)/shard_map/ppermute | solution.py:17
  182.9 5.5 %collective-permute-start.33 = (bf16[256,256]{1,0:T(8,128)(2,1)S(1)}, bf16[256,256]{1,0:T(8,128)(2,1)S(1)}, u32[]{:S(2)}, u32[]{:S(2)}) collective-permute-start(bf16[256,256]{1,0:T(8,128)(2,1)S(1)} %fusion.37), channel_id=1, source_target_pairs={{0,16},{8,24},{16,0},{24,8},{1,17},{9,25},{17,1},{25,9},{2,18},{10... | collective-permute-start | bytes 393224 | tf_op jit(solution)/shard_map/ppermute | solution.py:17
  184.8 6.8 %collective-permute-start.32 = (bf16[256,256]{1,0:T(8,128)(2,1)S(1)}, bf16[256,256]{1,0:T(8,128)(2,1)S(1)}, u32[]{:S(2)}, u32[]{:S(2)}) collective-permute-start(bf16[256,256]{1,0:T(8,128)(2,1)S(1)} %fusion.37), channel_id=1, source_target_pairs={{0,8},{8,0},{16,24},{24,16},{1,9},{9,1},{17,25},{25,17},{2,10},{10... | collective-permute-start | bytes 393224 | tf_op jit(solution)/shard_map/ppermute | solution.py:17
  (23 other events, 161.2 us)
